TPU v7x, 32 devices: a whole 2x2x4 slice. The times are simulated.
32 devices in a mesh: gx: 4 (over z), gz: 4 (over y, core), sa: 2 (over x).
Axes of the slice: x: 2, y: 2, z: 4, core: 2. Of those that a mesh axis runs over, the one named last changes fastest.
Arguments:
- forcing: float32 [3, 8, 128, 32, 256], P(None, 'sa', 'gx', 'gz'), may hold values from -60 to 60
- velocity: float32 [256], replicated, may hold values from 0.3 to 1.2
- wall_solve: float32 [256, 256], replicated, may hold values from -1 to 1.7
Outputs:
- basis: float32 [3, 8, 128, 32, 256], P(None, 'sa', 'gx', 'gz')
- factor: float32 [8, 8], replicated
All inputs are finite; a program needn't handle non-finite values.
Results may differ from a plain program's by a relative error of at most 0.00015.
Values sent between devices are 32-bit elements; how exact they have to be, the bound alone decides.
No kernel may reach another device: no remote copies, remote signals or barrier semaphores. Data moves between devices by JAX's collectives and lax.ppermute only.
A program may use at most 64 MiB of HBM per device.

v0:
```python
import jax
import jax.numpy as jnp
from jax import lax
from jax.sharding import PartitionSpec as P

step_length = 0.4
viscosity = 0.2


def extended(cells, sides, width):
    for axis, dim in sides:
        count = lax.axis_size(axis)
        head = lax.slice_in_dim(cells, 0, width, axis=dim)
        tail = lax.slice_in_dim(cells, cells.shape[dim] - width, cells.shape[dim], axis=dim)
        cells = jnp.concatenate(
            [
                lax.ppermute(tail, axis, [(i, (i + 1) % count) for i in range(count)]),
                cells,
                lax.ppermute(head, axis, [((i + 1) % count, i) for i in range(count)]),
            ],
            axis=dim,
        )
    return cells


def shear_of(velocity):
    inner = (velocity[2:] - velocity[:-2]) * 0.5
    return jnp.concatenate([velocity[1:2] - velocity[0:1], inner, velocity[-1:] - velocity[-2:-1]])


def upper_factor(gram):
    order_size = gram.shape[0]
    column_ids = jnp.arange(order_size)
    row_list = []
    for pivot_index in range(order_size):
        current_row = gram[pivot_index]
        for other_index in range(pivot_index):
            current_row = current_row - row_list[other_index][pivot_index] * row_list[other_index]
        current_row = jnp.where(
            column_ids >= pivot_index, current_row, jnp.zeros_like(current_row)
        ) / jnp.sqrt(current_row[pivot_index])
        row_list.append(current_row)
    return jnp.stack(row_list)


def upper_inverse(factor):
    order_size = factor.shape[0]
    identity_rows = jnp.eye(order_size, dtype=factor.dtype)
    row_list = [None] * order_size
    for pivot_index in range(order_size - 1, -1, -1):
        current_row = identity_rows[pivot_index]
        for other_index in range(pivot_index + 1, order_size):
            current_row = current_row - factor[pivot_index, other_index] * row_list[other_index]
        row_list[pivot_index] = current_row / factor[pivot_index, pivot_index]
    return jnp.stack(row_list)


def stencil(padded, velocity, shear_rate, adjoint):
    center = padded[:, :, 1:-1, 1:-1]
    east_side = padded[:, :, 2:, 1:-1]
    west_side = padded[:, :, :-2, 1:-1]
    north_side = padded[:, :, 1:-1, 2:]
    south_side = padded[:, :, 1:-1, :-2]
    direction = 1.0 if adjoint else -1.0
    change = direction * velocity * (east_side - west_side) * 0.5 + viscosity * (
        east_side + west_side + north_side + south_side - 4.0 * center
    )
    if adjoint:
        change = change.at[1].add(-shear_rate * center[0])
    else:
        change = change.at[0].add(-shear_rate * center[1])
    return (center, change)


def wall_apply(field, wall_solve):
    return jnp.matmul(field, wall_solve, precision=lax.Precision.HIGHEST)


def wall_adjoint(field, wall_solve):
    return jnp.matmul(field, wall_solve.T, precision=lax.Precision.HIGHEST)


def near_faces(field):
    return extended(field, (("gx", 2), ("gz", 3)), 1)


def shards(forcing, velocity, wall_solve):
    shear_rate = shear_of(velocity)
    columns = forcing.shape[1]
    entries = (
        3
        * forcing.shape[2]
        * lax.axis_size("gx")
        * forcing.shape[3]
        * lax.axis_size("gz")
        * forcing.shape[4]
    )
    current = forcing
    for repeat in range(2):
        center, change = stencil(near_faces(current), velocity, shear_rate, False)
        current = wall_apply(center + step_length * (change + forcing), wall_solve)
    partial_value = jnp.sum(current * current, axis=(0, 2, 3, 4))
    response = current
    current = response
    for repeat in range(2):
        solved = wall_adjoint(current, wall_solve)
        center, change = stencil(near_faces(solved), velocity, shear_rate, True)
        current = center + step_length * change + step_length * response
    gathered = lax.all_gather(current, "sa", axis=1, tiled=True)
    half_rows = gathered.shape[4] // lax.axis_size("sa")
    row_block = lax.dynamic_slice_in_dim(gathered, lax.axis_index("sa") * half_rows, half_rows, 4)
    gram_local = jnp.einsum(
        "cixzy,cjxzy->ij", row_block, row_block, precision=lax.Precision.HIGHEST
    )
    slot_norms = jnp.zeros((columns * lax.axis_size("sa"),), jnp.float32)
    slot_norms = lax.dynamic_update_slice_in_dim(
        slot_norms, partial_value, lax.axis_index("sa") * columns, 0
    )
    raw_gram, totals = lax.psum((gram_local, slot_norms), ("gx", "gz", "sa"))
    scale_all = jnp.sqrt(totals / entries + 1e-06)
    gram = raw_gram / entries / (scale_all[:, None] * scale_all[None, :])
    factor = upper_factor(gram)
    inverse = upper_inverse(factor)
    coefficient = inverse / scale_all[:, None]
    own_coef = lax.dynamic_slice_in_dim(coefficient, lax.axis_index("sa") * columns, columns, 1)
    basis_own = jnp.einsum("cixzy,ij->cjxzy", gathered, own_coef, precision=lax.Precision.HIGHEST)
    return (basis_own, factor)


def solution(mesh):
    return jax.shard_map(
        shards,
        mesh=mesh,
        in_specs=(P(None, "sa", "gx", "gz", None), P(), P()),
        out_specs=(P(None, "sa", "gx", "gz", None), P()),
        check_vma=False,
    )
```

profile of v0, /device:TPU:0, one launch (start us, length us, event | category | flops | bytes accessed | tf_op | source)
XLA Modules:
  0.0 341.3 jit_solution(7292808118564609644)
XLA Ops:
  8.2 3.1 collective-permute-start.1
  14.2 2.5 collective-permute-done.1
  22.2 6.5 %collective-permute-done.2 = f32[3,4,34,1,256]{4,3,2,1,0:T(1,128)S(1)} collective-permute-done((f32[3,4,34,1,256]{4,3,2,1,0:T(1,128)S(1)}, f32[3,4,34,1,256]{4,3,2,1,0:T(1,128)S(1)}, u32[]{:S(2)}, u32[]{:S(2)}) %collective-permute-start.2) | collective-permute-done | bytes 417824 | tf_op jit(solution)/shard_map/ppermute | solution.py:19
  28.7 3.0 collective-permute-done.3
  34.2 2.8 fusion.32
  37.0 3.4 collective-permute-start.4
  40.4 3.2 collective-permute-done.4
  43.6 3.2 collective-permute-done.5
  47.9 9.3 %collective-permute-done.6 = f32[3,4,34,1,256]{4,3,2,1,0:T(1,128)S(1)} collective-permute-done((f32[3,4,34,1,256]{4,3,2,1,0:T(1,128)S(1)}, f32[3,4,34,1,256]{4,3,2,1,0:T(1,128)S(1)}, u32[]{:S(2)}, u32[]{:S(2)}) %collective-permute-start.6) | collective-permute-done | bytes 417824 | tf_op jit(solution)/shard_map/ppermute | solution.py:19
  58.4 2.4 fusion.15
  61.1 2.9 fusion.28
  64.0 2.8 fusion.54
  69.0 3.6 %collective-permute-done.8 = f32[3,4,1,8,256]{4,3,2,1,0:T(8,128)S(1)} collective-permute-done((f32[3,4,1,8,256]{4,3,2,1,0:T(8,128)S(1)}, f32[3,4,1,8,256]{4,3,2,1,0:T(8,128)S(1)}, u32[]{:S(2)}, u32[]{:S(2)}) %collective-permute-start.8) | collective-permute-done | bytes 98336 | tf_op jit(solution)/shard_map/ppermute | solution.py:19
  75.1 8.5 %collective-permute-done.10 = f32[3,4,34,1,256]{4,3,2,1,0:T(1,128)S(1)} collective-permute-done((f32[3,4,34,1,256]{4,3,2,1,0:T(1,128)S(1)}, f32[3,4,34,1,256]{4,3,2,1,0:T(1,128)S(1)}, u32[]{:S(2)}, u32[]{:S(2)}) %collective-permute-start.10) | collective-permute-done | bytes 417824 | tf_op jit(solution)/shard_map/ppermute | solution.py:19
  83.5 3.0 collective-permute-done.11
  89.2 3.0 fusion.24
  94.2 2.8 collective-permute-done.12
  97.0 2.6 collective-permute-done.13
  100.8 9.1 %collective-permute-done.14 = f32[3,4,34,1,256]{4,3,2,1,0:T(1,128)S(1)} collective-permute-done((f32[3,4,34,1,256]{4,3,2,1,0:T(1,128)S(1)}, f32[3,4,34,1,256]{4,3,2,1,0:T(1,128)S(1)}, u32[]{:S(2)}, u32[]{:S(2)}) %collective-permute-start.14) | collective-permute-done | bytes 417824 | tf_op jit(solution)/shard_map/ppermute | solution.py:19
  109.9 2.4 collective-permute-done.15
  112.3 2.4 fusion.5
  115.0 2.5 multiply_reduce_fusion
  117.9 78.3 %all-gather.2.cloned.1.call-done = f32[3,8,32,8,256]{4,3,2,1,0:T(8,128)} async-done(((f32[3,4,32,8,256]{4,3,2,1,0:T(8,128)}), f32[3,8,32,8,256]{4,3,2,1,0:T(8,128)}) %all-gather.2.cloned.1.call-update) | async-done | bytes 6291472 | tf_op jit(solution)/shard_map/all_gather | solution.py:109
  198.2 7.5 %fusion.43 = f32[8,8]{1,0:T(8,128)S(1)} fusion(f32[3,8,32,8,128]{4,3,2,1,0:T(8,128)S(1)} %constant_dynamic-slice_fusion), kind=kOutput, calls=%fused_computation.71 | convolution fusion | flops 75497472 | bytes 3145984 | tf_op jit(solution)/shard_map/cixzy,cjxzy->ij/dot_general | solution.py:112
  205.7 39.6 %all-reduce = (f32[8,8]{1,0:T(8,128)S(1)}, f32[8]{0:T(128)S(1)}) all-reduce(f32[8,8]{1,0:T(8,128)S(1)} %fusion.43, f32[8]{0:T(128)S(1)} %dynamic_update_slice.3), channel_id=1, replica_groups=mesh['gx'=4,'gz'=4,'sa'=2] {'gx','gz','sa'}, use_global_device_ids=true, to_apply=%region_0.0 | all-reduce | flops 72 | bytes 576 | tf_op jit(solution)/shard_map/psum | solution.py:119
  257.0 2.5 fusion.85
  261.5 3.1 fusion.83
  266.5 3.8 %multiply_subtract_fusion.2 = f32[8]{0:T(128)S(1)} fusion(f32[]{:T(128)} %bitcast.40, f32[]{:T(128)} %bitcast.39, f32[]{:T(128)} %bitcast.38, f32[]{:T(128)} %bitcast.37, f32[]{:T(128)} %bitcast.36, f32[]{:T(128)} %bitcast.35, f32[8,8]{1,0:T(8,128)S(1)} %multiply_divide_fusion, f32[]{:T(128)} %bitcast.33, f32[8]{0:T(128)S(1)} %fusion.83, f32[]{:T(128)} %bitcast.25, ...), kind=kLoop, calls=%fused_computation.164 | loop fusion | flops 224 | bytes 304 | tf_op jit(solution)/shard_map/sub | solution.py:38
  272.3 4.6 %multiply_subtract_fusion = f32[8]{0:T(128)S(1)} fusion(f32[]{:T(128)} %bitcast.50, f32[]{:T(128)} %bitcast.49, f32[]{:T(128)} %bitcast.48, f32[]{:T(128)} %bitcast.47, f32[]{:T(128)} %bitcast.46, f32[]{:T(128)} %bitcast.45, f32[]{:T(128)} %bitcast.44, f32[8,8]{1,0:T(8,128)S(1)} %multiply_divide_fusion, f32[]{:T(128)} %bitcast.42, ...), kind=kLoop, calls=%fused_computation.161 | loop fusion | flops 264 | bytes 344 | tf_op jit(solution)/shard_map/sub | solution.py:38
  278.1 16.9 %fusion.73 = (f32[1,8]{1,0:T(1,128)S(1)}, f32[1,8]{1,0:T(1,128)S(1)}, f32[1,8]{1,0:T(1,128)S(1)}, f32[1,8]{1,0:T(1,128)S(1)}, f32[1,8]{1,0:T(1,128)S(1)}, /*index=5*/f32[1,8]{1,0:T(1,128)S(1)}, f32[1,8]{1,0:T(1,128)S(1)}) fusion(f32[]{:T(128)} %bitcast.52, f32[]{:T(128)} %bitcast.50, f32[]{:T(128)} %bitcast.49, f32[]{:T(128)} %bitcast.48, f32[]{:T(128)} %bitcast.47, ...), kind=kLoop, calls=%fused_computation.134 | loop fusion | flops 608 | bytes 620 | tf_op jit(solution)/shard_map/div | solution.py:39
  298.3 22.7 %subtract_divide_fusion = (f32[1,8]{1,0:T(1,128)S(1)}, f32[1,8]{1,0:T(1,128)S(1)}, f32[1,8]{1,0:T(1,128)S(1)}, f32[1,8]{1,0:T(1,128)S(1)}, f32[1,8]{1,0:T(1,128)...) fusion(f32[8,8]{1,0:T(8,128)S(1)} %fusion.60, f32[]{:T(128)} %bitcast.75, f32[]{:T(128)} %bitcast.44, ...), kind=kLoop, calls=%fused_computation.154 | loop fusion | flops 512 | bytes 656 | tf_op jit(solution)/shard_map/div | solution.py:54
  321.1 11.2 %fusion.37 = f32[3,4,32,8,256]{4,1,3,2,0:T(4,128)S(1)} fusion(f32[3,8,32,8,256]{4,3,2,1,0:T(8,128)} %all-gather.2.cloned.1.call-done, f32[8,8]{1,0:T(8,128)S(1)} %broadcast_divide_fusion, s32[]{:T(128)S(6)} %select_n.71), kind=kOutput, calls=%fused_computation.67 | convolution fusion | flops 75497472 | bytes 9437444 | tf_op jit(solution)/shard_map/cixzy,ij->cjxzy/dot_general | solution.py:126
  (85 shorter events, 46.2 us)
Async XLA Ops:
  7.2 27.0 %copy-start = (f32[256,256]{1,0:T(8,128)S(1)}, f32[256,256]{1,0:T(8,128)}, u32[]{:S(2)}) copy-start(f32[256,256]{1,0:T(8,128)} %param.13) | copy-start | bytes 786436
  7.2 188.9 %all-gather.2.cloned.1.call-start = ((), (), s32[]{:S(2)}) async-start(), calls=%async_computation | async-start | bytes 9437184 | tf_op jit(solution)/shard_map/all_gather | solution.py:109
  8.2 8.6 %collective-permute-start.1 = (f32[3,4,1,8,256]{4,3,2,1,0:T(8,128)S(1)}, f32[3,4,1,8,256]{4,3,2,1,0:T(8,128)S(1)}, u32[]{:S(2)}, u32[]{:S(2)}) collective-permute-start(f32[3,4,1,8,256]{4,3,2,1,0:T(8,128)S(1)} %get-tuple-element.86), channel_id=1, source_target_pairs={{0,8},{8,16},{16,24},{24,0},{1,9},{9,17},{17,25},{25,1},{2,10},{10... | collective-permute-start | bytes 294920 | tf_op jit(solution)/shard_map/ppermute | solution.py:17
  11.3 7.8 %collective-permute-start = (f32[3,4,1,8,256]{4,3,2,1,0:T(8,128)S(1)}, f32[3,4,1,8,256]{4,3,2,1,0:T(8,128)S(1)}, u32[]{:S(2)}, u32[]{:S(2)}) collective-permute-start(f32[3,4,1,8,256]{4,3,2,1,0:T(8,128)S(1)} %get-tuple-element.85), channel_id=1, source_target_pairs={{8,0},{16,8},{24,16},{0,24},{9,1},{17,9},{25,17},{1,25},{10,2},{18... | collective-permute-start | bytes 294920 | tf_op jit(solution)/shard_map/ppermute | solution.py:19
  16.8 3.4 copy-start.2
  16.8 14.8 %copy-start.1 = (f32[3,4,32,8,256]{4,3,2,1,0:T(8,128)S(1)}, f32[3,4,32,8,256]{4,3,2,1,0:T(8,128)}, u32[]{:S(2)}) copy-start(f32[3,4,32,8,256]{4,3,2,1,0:T(8,128)} %param.11) | copy-start | bytes 9437188
  19.6 9.0 %collective-permute-start.2 = (f32[3,4,34,1,256]{4,3,2,1,0:T(1,128)S(1)}, f32[3,4,34,1,256]{4,3,2,1,0:T(1,128)S(1)}, u32[]{:S(2)}, u32[]{:S(2)}) collective-permute-start(f32[3,4,34,1,256]{4,3,2,1,0:T(1,128)S(1)} %get-tuple-element.75), channel_id=1, source_target_pairs={{2,0},{4,2},{6,4},{0,6},{3,1},{5,3},{7,5},{1,7},{10,8},{12,10},{14... | collective-permute-start | bytes 1253384 | tf_op jit(solution)/shard_map/ppermute | solution.py:19
  19.7 11.9 %collective-permute-start.3 = (f32[3,4,34,1,256]{4,3,2,1,0:T(1,128)S(1)}, f32[3,4,34,1,256]{4,3,2,1,0:T(1,128)S(1)}, u32[]{:S(2)}, u32[]{:S(2)}) collective-permute-start(f32[3,4,34,1,256]{4,3,2,1,0:T(1,128)S(1)} %get-tuple-element.76), channel_id=1, source_target_pairs={{0,2},{2,4},{4,6},{6,0},{1,3},{3,5},{5,7},{7,1},{8,10},{10,12},{12... | collective-permute-start | bytes 1253384 | tf_op jit(solution)/shard_map/ppermute | solution.py:17
  37.0 6.6 %collective-permute-start.4 = (f32[3,4,1,8,256]{4,3,2,1,0:T(8,128)S(1)}, f32[3,4,1,8,256]{4,3,2,1,0:T(8,128)S(1)}, u32[]{:S(2)}, u32[]{:S(2)}) collective-permute-start(f32[3,4,1,8,256]{4,3,2,1,0:T(8,128)S(1)} %get-tuple-element.84), channel_id=1, source_target_pairs={{8,0},{16,8},{24,16},{0,24},{9,1},{17,9},{25,17},{1,25},{10,2},{18... | collective-permute-start | bytes 294920 | tf_op jit(solution)/shard_map/ppermute | solution.py:19
  40.4 6.4 %collective-permute-start.5 = (f32[3,4,1,8,256]{4,3,2,1,0:T(8,128)S(1)}, f32[3,4,1,8,256]{4,3,2,1,0:T(8,128)S(1)}, u32[]{:S(2)}, u32[]{:S(2)}) collective-permute-start(f32[3,4,1,8,256]{4,3,2,1,0:T(8,128)S(1)} %get-tuple-element.83), channel_id=1, source_target_pairs={{0,8},{8,16},{16,24},{24,0},{1,9},{9,17},{17,25},{25,1},{2,10},{10... | collective-permute-start | bytes 294920 | tf_op jit(solution)/shard_map/ppermute | solution.py:17
  47.3 9.9 %collective-permute-start.6 = (f32[3,4,34,1,256]{4,3,2,1,0:T(1,128)S(1)}, f32[3,4,34,1,256]{4,3,2,1,0:T(1,128)S(1)}, u32[]{:S(2)}, u32[]{:S(2)}) collective-permute-start(f32[3,4,34,1,256]{4,3,2,1,0:T(1,128)S(1)} %get-tuple-element.73), channel_id=1, source_target_pairs={{2,0},{4,2},{6,4},{0,6},{3,1},{5,3},{7,5},{1,7},{10,8},{12,10},{14... | collective-permute-start | bytes 1253384 | tf_op jit(solution)/shard_map/ppermute | solution.py:19
  47.4 11.0 %collective-permute-start.7 = (f32[3,4,34,1,256]{4,3,2,1,0:T(1,128)S(1)}, f32[3,4,34,1,256]{4,3,2,1,0:T(1,128)S(1)}, u32[]{:S(2)}, u32[]{:S(2)}) collective-permute-start(f32[3,4,34,1,256]{4,3,2,1,0:T(1,128)S(1)} %get-tuple-element.74), channel_id=1, source_target_pairs={{0,2},{2,4},{4,6},{6,0},{1,3},{3,5},{5,7},{7,1},{8,10},{10,12},{12... | collective-permute-start | bytes 1253384 | tf_op jit(solution)/shard_map/ppermute | solution.py:17
  66.9 5.7 %collective-permute-start.8 = (f32[3,4,1,8,256]{4,3,2,1,0:T(8,128)S(1)}, f32[3,4,1,8,256]{4,3,2,1,0:T(8,128)S(1)}, u32[]{:S(2)}, u32[]{:S(2)}) collective-permute-start(f32[3,4,1,8,256]{4,3,2,1,0:T(8,128)S(1)} %get-tuple-element.82), channel_id=1, source_target_pairs={{8,0},{16,8},{24,16},{0,24},{9,1},{17,9},{25,17},{1,25},{10,2},{18... | collective-permute-start | bytes 294920 | tf_op jit(solution)/shard_map/ppermute | solution.py:19
  67.5 6.5 %collective-permute-start.9 = (f32[3,4,1,8,256]{4,3,2,1,0:T(8,128)S(1)}, f32[3,4,1,8,256]{4,3,2,1,0:T(8,128)S(1)}, u32[]{:S(2)}, u32[]{:S(2)}) collective-permute-start(f32[3,4,1,8,256]{4,3,2,1,0:T(8,128)S(1)} %get-tuple-element.81), channel_id=1, source_target_pairs={{0,8},{8,16},{16,24},{24,0},{1,9},{9,17},{17,25},{25,1},{2,10},{10... | collective-permute-start | bytes 294920 | tf_op jit(solution)/shard_map/ppermute | solution.py:17
  74.5 9.0 %collective-permute-start.10 = (f32[3,4,34,1,256]{4,3,2,1,0:T(1,128)S(1)}, f32[3,4,34,1,256]{4,3,2,1,0:T(1,128)S(1)}, u32[]{:S(2)}, u32[]{:S(2)}) collective-permute-start(f32[3,4,34,1,256]{4,3,2,1,0:T(1,128)S(1)} %get-tuple-element.71), channel_id=1, source_target_pairs={{2,0},{4,2},{6,4},{0,6},{3,1},{5,3},{7,5},{1,7},{10,8},{12,10},{14... | collective-permute-start | bytes 1253384 | tf_op jit(solution)/shard_map/ppermute | solution.py:19
  74.6 11.9 %collective-permute-start.11 = (f32[3,4,34,1,256]{4,3,2,1,0:T(1,128)S(1)}, f32[3,4,34,1,256]{4,3,2,1,0:T(1,128)S(1)}, u32[]{:S(2)}, u32[]{:S(2)}) collective-permute-start(f32[3,4,34,1,256]{4,3,2,1,0:T(1,128)S(1)} %get-tuple-element.72), channel_id=1, source_target_pairs={{0,2},{2,4},{4,6},{6,0},{1,3},{3,5},{5,7},{7,1},{8,10},{10,12},{12... | collective-permute-start | bytes 1253384 | tf_op jit(solution)/shard_map/ppermute | solution.py:17
  92.2 4.9 %collective-permute-start.12 = (f32[3,4,1,8,256]{4,3,2,1,0:T(8,128)S(1)}, f32[3,4,1,8,256]{4,3,2,1,0:T(8,128)S(1)}, u32[]{:S(2)}, u32[]{:S(2)}) collective-permute-start(f32[3,4,1,8,256]{4,3,2,1,0:T(8,128)S(1)} %get-tuple-element.80), channel_id=1, source_target_pairs={{8,0},{16,8},{24,16},{0,24},{9,1},{17,9},{25,17},{1,25},{10,2},{18... | collective-permute-start | bytes 294920 | tf_op jit(solution)/shard_map/ppermute | solution.py:19
  93.1 6.6 %collective-permute-start.13 = (f32[3,4,1,8,256]{4,3,2,1,0:T(8,128)S(1)}, f32[3,4,1,8,256]{4,3,2,1,0:T(8,128)S(1)}, u32[]{:S(2)}, u32[]{:S(2)}) collective-permute-start(f32[3,4,1,8,256]{4,3,2,1,0:T(8,128)S(1)} %get-tuple-element.79), channel_id=1, source_target_pairs={{0,8},{8,16},{16,24},{24,0},{1,9},{9,17},{17,25},{25,1},{2,10},{10... | collective-permute-start | bytes 294920 | tf_op jit(solution)/shard_map/ppermute | solution.py:17
  100.2 9.7 %collective-permute-start.14 = (f32[3,4,34,1,256]{4,3,2,1,0:T(1,128)S(1)}, f32[3,4,34,1,256]{4,3,2,1,0:T(1,128)S(1)}, u32[]{:S(2)}, u32[]{:S(2)}) collective-permute-start(f32[3,4,34,1,256]{4,3,2,1,0:T(1,128)S(1)} %get-tuple-element.69), channel_id=1, source_target_pairs={{2,0},{4,2},{6,4},{0,6},{3,1},{5,3},{7,5},{1,7},{10,8},{12,10},{14... | collective-permute-start | bytes 1253384 | tf_op jit(solution)/shard_map/ppermute | solution.py:19
  100.6 11.7 %collective-permute-start.15 = (f32[3,4,34,1,256]{4,3,2,1,0:T(1,128)S(1)}, f32[3,4,34,1,256]{4,3,2,1,0:T(1,128)S(1)}, u32[]{:S(2)}, u32[]{:S(2)}) collective-permute-start(f32[3,4,34,1,256]{4,3,2,1,0:T(1,128)S(1)} %get-tuple-element.70), channel_id=1, source_target_pairs={{0,2},{2,4},{4,6},{6,0},{1,3},{3,5},{5,7},{7,1},{8,10},{10,12},{12... | collective-permute-start | bytes 1253384 | tf_op jit(solution)/shard_map/ppermute | solution.py:17
Sparse Core Ops, SparseCore 0:
  117.7 78.3 all-gather.1
where the time goes:
time: 342 us; the launch traced here: 341 us
  waiting for transfers between devices  141 us (41%)
  other arithmetic  74.8 us (22%)
  blocking collectives  39.6 us (12%)
  matrix products  30.2 us (9%)
  local copies, waits for them, and re-layouts  21.2 us (6%)
  between operations  19.9 us (6%)
  starting transfers between devices  15 us (4%)
    all_gather x1, waiting for transfers between devices, shards(): gathered = lax.all_gather(current, 'sa', axis=1, tiled=True)  78.3 us
    ppermute x8, waiting for transfers between devices, extended(): lax.ppermute(head, axis, [((i + 1) % count, i) for i in range(count)])  43.1 us
    psum x1, blocking collectives, shards(): raw_gram, totals = lax.psum((gram_local, slot_norms), ('gx', 'gz', 'sa'))  39.6 us
    div x1, other arithmetic, upper_inverse(): row_list[pivot_index] = current_row / factor[pivot_index, pivot_index]  22.7 us
    ppermute x8, waiting for transfers between devices, extended(): lax.ppermute(tail, axis, [(i, (i + 1) % count) for i in range(count)])  19.3 us
    sub x7, other arithmetic, upper_factor(): current_row - row_list[other_index][pivot_index] * row_list[other_index]  17.6 us
    div x8, other arithmetic, upper_factor(): jnp.where(column_ids >= pivot_index, current_row, jnp.zeros_like(current_...  17 us
    dot_general x1, matrix products, shards(): jnp.einsum('cixzy,ij->cjxzy', gathered, own_coef, precision=lax.Precision...  11.2 us
  transfers between devices with their start and end apart: 17, of which 16 were waited for; matrix products, arithmetic and copies ran while one was open for 2% of the time, Pallas kernels for 0%

commit v1 on v0

--- a/solution.py
+++ b/solution.py
@@ -106,7 +106,20 @@
         solved = wall_adjoint(current, wall_solve)
         center, change = stencil(near_faces(solved), velocity, shear_rate, True)
         current = center + step_length * change + step_length * response
-    gathered = lax.all_gather(current, "sa", axis=1, tiled=True)
+    kept_arr, answer, upper = (lax.axis_size("sa"), lax.axis_index("sa"), current.shape[1])
+    vec_out, after = (current, 1)
+    while after < kept_arr:
+        vec_out = jnp.concatenate(
+            [
+                vec_out,
+                lax.ppermute(
+                    vec_out, "sa", tuple(((h, (h - after) % kept_arr) for h in range(kept_arr)))
+                ),
+            ],
+            axis=1,
+        )
+        after = 2 * after
+    gathered = jnp.roll(vec_out, answer * upper, axis=1)
     half_rows = gathered.shape[4] // lax.axis_size("sa")
     row_block = lax.dynamic_slice_in_dim(gathered, lax.axis_index("sa") * half_rows, half_rows, 4)
     gram_local = jnp.einsum(

time: 342 us -> 330 us (0.965)
  between operations: 19.9 us -> 6.12 us
  waiting for transfers between devices: 141 us -> 131 us
  local copies, waits for them, and re-layouts: 21.2 us -> 30 us
    all_gather x1 -> x0, waiting for transfers between devices: 78.3 us -> none  [shards(): gathered = lax.all_gather(current, 'sa', axis=1, tiled=True)]
    ppermute x0 -> x1, waiting for transfers between devices: none -> 68.3 us  [shards(): lax.ppermute(vec_out, 'sa', tuple(((h, (h - after) % kept_arr) for h in r...]
    dynamic_slice x0 -> x1, local copies, waits for them, and re-layouts: none -> 6.01 us  [shards(): gathered = jnp.roll(vec_out, answer * upper, axis=1)]
    concatenate x0 -> x1, other arithmetic: none -> 4.7 us  [shards(): gathered = jnp.roll(vec_out, answer * upper, axis=1)]
    unnamed x9 -> x13, local copies, waits for them, and re-layouts: 4.5 us -> 9.01 us
where the time goes in v1:
time: 330 us; the launch traced here: 329 us
  waiting for transfers between devices  131 us (40%)
  other arithmetic  77.1 us (23%)
  blocking collectives  38.2 us (12%)
  matrix products  30.3 us (9%)
  local copies, waits for them, and re-layouts  30 us (9%)
  starting transfers between devices  16.5 us (5%)
  between operations  6.12 us (2%)
    ppermute x1, waiting for transfers between devices, shards(): lax.ppermute(vec_out, 'sa', tuple(((h, (h - after) % kept_arr) for h in r...  68.3 us
    ppermute x8, waiting for transfers between devices, extended(): lax.ppermute(head, axis, [((i + 1) % count, i) for i in range(count)])  43.1 us
    psum x1, blocking collectives, shards(): raw_gram, totals = lax.psum((gram_local, slot_norms), ('gx', 'gz', 'sa'))  38.2 us
    div x1, other arithmetic, upper_inverse(): row_list[pivot_index] = current_row / factor[pivot_index, pivot_index]  22.2 us
    ppermute x8, waiting for transfers between devices, extended(): lax.ppermute(tail, axis, [(i, (i + 1) % count) for i in range(count)])  19.3 us
    sub x7, other arithmetic, upper_factor(): current_row - row_list[other_index][pivot_index] * row_list[other_index]  17.5 us
    div x8, other arithmetic, upper_factor(): jnp.where(column_ids >= pivot_index, current_row, jnp.zeros_like(current_...  16.8 us
    dot_general x1, matrix products, shards(): jnp.einsum('cixzy,ij->cjxzy', gathered, own_coef, precision=lax.Precision...  11.3 us
  transfers between devices with their start and end apart: 17, of which 16 were waited for; matrix products, arithmetic and copies ran while one was open for 2% of the time, Pallas kernels for 0%

profile of v1, /device:TPU:0, one launch (start us, length us, event | category | flops | bytes accessed | tf_op | source)
XLA Modules:
  0.0 329.0 jit_solution(12279312556103069162)
XLA Ops:
  1.6 3.1 collective-permute-start.1
  7.7 2.5 collective-permute-done.1
  15.6 6.5 %collective-permute-done.2 = f32[3,4,34,1,256]{4,3,2,1,0:T(1,128)S(1)} collective-permute-done((f32[3,4,34,1,256]{4,3,2,1,0:T(1,128)S(1)}, f32[3,4,34,1,256]{4,3,2,1,0:T(1,128)S(1)}, u32[]{:S(2)}, u32[]{:S(2)}) %collective-permute-start.2) | collective-permute-done | bytes 417824 | tf_op jit(solution)/shard_map/ppermute | solution.py:19
  22.1 3.0 collective-permute-done.3
  27.6 2.8 fusion.32
  30.5 3.4 %collective-permute-start.4 = (f32[3,4,1,8,256]{4,3,2,1,0:T(8,128)S(1)}, f32[3,4,1,8,256]{4,3,2,1,0:T(8,128)S(1)}, u32[]{:S(2)}, u32[]{:S(2)}) collective-permute-start(f32[3,4,1,8,256]{4,3,2,1,0:T(8,128)S(1)} %get-tuple-element.84), channel_id=1, source_target_pairs={{8,0},{16,8},{24,16},{0,24},{9,1},{17,9},{25,17},{1,25},{10,2},{18... | collective-permute-start | bytes 294920 | tf_op jit(solution)/shard_map/ppermute | solution.py:19
  33.9 3.2 collective-permute-done.4
  37.0 3.2 collective-permute-done.5
  41.3 9.3 %collective-permute-done.6 = f32[3,4,34,1,256]{4,3,2,1,0:T(1,128)S(1)} collective-permute-done((f32[3,4,34,1,256]{4,3,2,1,0:T(1,128)S(1)}, f32[3,4,34,1,256]{4,3,2,1,0:T(1,128)S(1)}, u32[]{:S(2)}, u32[]{:S(2)}) %collective-permute-start.6) | collective-permute-done | bytes 417824 | tf_op jit(solution)/shard_map/ppermute | solution.py:19
  54.6 2.9 fusion.28
  57.5 2.8 fusion.54
  62.4 3.6 %collective-permute-done.8 = f32[3,4,1,8,256]{4,3,2,1,0:T(8,128)S(1)} collective-permute-done((f32[3,4,1,8,256]{4,3,2,1,0:T(8,128)S(1)}, f32[3,4,1,8,256]{4,3,2,1,0:T(8,128)S(1)}, u32[]{:S(2)}, u32[]{:S(2)}) %collective-permute-start.8) | collective-permute-done | bytes 98336 | tf_op jit(solution)/shard_map/ppermute | solution.py:19
  68.5 8.5 %collective-permute-done.10 = f32[3,4,34,1,256]{4,3,2,1,0:T(1,128)S(1)} collective-permute-done((f32[3,4,34,1,256]{4,3,2,1,0:T(1,128)S(1)}, f32[3,4,34,1,256]{4,3,2,1,0:T(1,128)S(1)}, u32[]{:S(2)}, u32[]{:S(2)}) %collective-permute-start.10) | collective-permute-done | bytes 417824 | tf_op jit(solution)/shard_map/ppermute | solution.py:19
  76.9 3.0 collective-permute-done.11
  82.6 3.0 fusion.24
  87.7 2.8 collective-permute-done.12
  90.5 2.7 collective-permute-done.13
  94.2 9.1 %collective-permute-done.14 = f32[3,4,34,1,256]{4,3,2,1,0:T(1,128)S(1)} collective-permute-done((f32[3,4,34,1,256]{4,3,2,1,0:T(1,128)S(1)}, f32[3,4,34,1,256]{4,3,2,1,0:T(1,128)S(1)}, u32[]{:S(2)}, u32[]{:S(2)}) %collective-permute-start.14) | collective-permute-done | bytes 417824 | tf_op jit(solution)/shard_map/ppermute | solution.py:19
  103.3 2.4 collective-permute-done.15
  111.1 68.3 %collective-permute-done.16 = f32[3,4,32,8,256]{4,3,2,1,0:T(8,128)} collective-permute-done((f32[3,4,32,8,256]{4,3,2,1,0:T(8,128)S(1)}, f32[3,4,32,8,256]{4,3,2,1,0:T(8,128)}, u32[]{:S(2)}, u32[]{:S(2)}) %collective-permute-start.16) | collective-permute-done | bytes 3145760 | tf_op jit(solution)/shard_map/ppermute | solution.py:115
  179.4 4.7 %pad_maximum_fusion = f32[3,16,32,8,256]{4,3,2,1,0:T(8,128)S(1)} fusion(f32[3,4,32,8,256]{4,3,2,1,0:T(8,128)} %collective-permute-done.16, f32[3,4,32,8,256]{4,3,2,1,0:T(8,128)S(1)} %get-tuple-element.78), kind=kLoop, calls=%fused_computation | loop fusion | flops 9437184 | bytes 18874368 | tf_op jit(solution)/shard_map/jit(_roll_dynamic)/concatenate | solution.py:122
  184.1 4.5 %copy-done.3 = f32[3,16,32,8,256]{4,3,2,1,0:T(8,128)} copy-done((f32[3,16,32,8,256]{4,3,2,1,0:T(8,128)}, f32[3,16,32,8,256]{4,3,2,1,0:T(8,128)S(1)}, u32[]{:S(2)}) %copy-start.3) | copy-done | bytes 12582936
  189.5 7.5 %fusion.43 = f32[8,8]{1,0:T(8,128)S(1)} fusion(f32[3,8,32,8,128]{4,3,2,1,0:T(8,128)S(1)} %constant_dynamic-slice_fusion.1), kind=kOutput, calls=%fused_computation.72 | convolution fusion | flops 75497472 | bytes 3145984 | tf_op jit(solution)/shard_map/cixzy,cjxzy->ij/dot_general | solution.py:125
  197.0 38.2 %all-reduce = (f32[8,8]{1,0:T(8,128)S(1)}, f32[8]{0:T(128)S(1)}) all-reduce(f32[8,8]{1,0:T(8,128)S(1)} %fusion.43, f32[8]{0:T(128)S(1)} %dynamic_update_slice.3), channel_id=1, replica_groups=mesh['gx'=4,'gz'=4,'sa'=2] {'gx','gz','sa'}, use_global_device_ids=true, to_apply=%region_0.0 | all-reduce | flops 72 | bytes 576 | tf_op jit(solution)/shard_map/psum | solution.py:132
  246.8 2.6 fusion.85
  251.3 3.2 fusion.83
  256.3 3.7 %multiply_subtract_fusion.2 = f32[8]{0:T(128)S(1)} fusion(f32[]{:T(128)} %bitcast.40, f32[]{:T(128)} %bitcast.39, f32[]{:T(128)} %bitcast.38, f32[]{:T(128)} %bitcast.37, f32[]{:T(128)} %bitcast.36, f32[]{:T(128)} %bitcast.35, f32[8,8]{1,0:T(8,128)S(1)} %multiply_divide_fusion, f32[]{:T(128)} %bitcast.33, f32[8]{0:T(128)S(1)} %fusion.83, f32[]{:T(128)} %bitcast.25, ...), kind=kLoop, calls=%fused_computation.166 | loop fusion | flops 224 | bytes 304 | tf_op jit(solution)/shard_map/sub | solution.py:38
  261.7 4.2 %multiply_subtract_fusion = f32[8]{0:T(128)S(1)} fusion(f32[]{:T(128)} %bitcast.50, f32[]{:T(128)} %bitcast.49, f32[]{:T(128)} %bitcast.48, f32[]{:T(128)} %bitcast.47, f32[]{:T(128)} %bitcast.46, f32[]{:T(128)} %bitcast.45, f32[]{:T(128)} %bitcast.44, f32[8,8]{1,0:T(8,128)S(1)} %multiply_divide_fusion, f32[]{:T(128)} %bitcast.42, ...), kind=kLoop, calls=%fused_computation.163 | loop fusion | flops 264 | bytes 344 | tf_op jit(solution)/shard_map/sub | solution.py:38
  267.1 16.8 %fusion.73 = (f32[1,8]{1,0:T(1,128)S(1)}, f32[1,8]{1,0:T(1,128)S(1)}, f32[1,8]{1,0:T(1,128)S(1)}, f32[1,8]{1,0:T(1,128)S(1)}, f32[1,8]{1,0:T(1,128)S(1)}, /*index=5*/f32[1,8]{1,0:T(1,128)S(1)}, f32[1,8]{1,0:T(1,128)S(1)}) fusion(f32[]{:T(128)} %bitcast.52, f32[]{:T(128)} %bitcast.50, f32[]{:T(128)} %bitcast.49, f32[]{:T(128)} %bitcast.48, f32[]{:T(128)} %bitcast.47, ...), kind=kLoop, calls=%fused_computation.136 | loop fusion | flops 608 | bytes 620 | tf_op jit(solution)/shard_map/div | solution.py:39
  287.1 6.0 %constant_dynamic-slice_fusion = f32[3,8,32,8,256]{4,3,2,1,0:T(8,128)} fusion(f32[3,16,32,8,256]{4,3,2,1,0:T(8,128)} %copy-done.3, s32[]{:T(128)S(6)} %select_n.88), kind=kLoop, calls=%fused_computation.120 | loop fusion | bytes 12582916 | tf_op jit(solution)/shard_map/jit(_roll_dynamic)/dynamic_slice | solution.py:122
  293.1 22.2 %subtract_divide_fusion = (f32[1,8]{1,0:T(1,128)S(1)}, f32[1,8]{1,0:T(1,128)S(1)}, f32[1,8]{1,0:T(1,128)S(1)}, f32[1,8]{1,0:T(1,128)S(1)}, f32[1,8]{1,0:T(1,128)...) fusion(f32[8,8]{1,0:T(8,128)S(1)} %fusion.60, f32[]{:T(128)} %bitcast.75, f32[]{:T(128)} %bitcast.44, ...), kind=kLoop, calls=%fused_computation.156 | loop fusion | flops 512 | bytes 656 | tf_op jit(solution)/shard_map/div | solution.py:54
  315.5 11.3 %fusion.37 = f32[3,4,32,8,256]{4,1,3,2,0:T(4,128)S(1)} fusion(f32[3,8,32,8,256]{4,3,2,1,0:T(8,128)} %constant_dynamic-slice_fusion, f32[8,8]{1,0:T(8,128)S(1)} %broadcast_divide_fusion, s32[]{:T(128)S(6)} %select_n.92), kind=kOutput, calls=%fused_computation.68 | convolution fusion | flops 75497472 | bytes 9437444 | tf_op jit(solution)/shard_map/cixzy,ij->cjxzy/dot_general | solution.py:139
  (90 shorter events, 51.8 us)
Async XLA Ops:
  0.6 27.0 %copy-start = (f32[256,256]{1,0:T(8,128)S(1)}, f32[256,256]{1,0:T(8,128)}, u32[]{:S(2)}) copy-start(f32[256,256]{1,0:T(8,128)} %param.13) | copy-start | bytes 786436
  1.6 8.6 %collective-permute-start.1 = (f32[3,4,1,8,256]{4,3,2,1,0:T(8,128)S(1)}, f32[3,4,1,8,256]{4,3,2,1,0:T(8,128)S(1)}, u32[]{:S(2)}, u32[]{:S(2)}) collective-permute-start(f32[3,4,1,8,256]{4,3,2,1,0:T(8,128)S(1)} %get-tuple-element.86), channel_id=1, source_target_pairs={{0,8},{8,16},{16,24},{24,0},{1,9},{9,17},{17,25},{25,1},{2,10},{10... | collective-permute-start | bytes 294920 | tf_op jit(solution)/shard_map/ppermute | solution.py:17
  4.8 7.8 %collective-permute-start = (f32[3,4,1,8,256]{4,3,2,1,0:T(8,128)S(1)}, f32[3,4,1,8,256]{4,3,2,1,0:T(8,128)S(1)}, u32[]{:S(2)}, u32[]{:S(2)}) collective-permute-start(f32[3,4,1,8,256]{4,3,2,1,0:T(8,128)S(1)} %get-tuple-element.85), channel_id=1, source_target_pairs={{8,0},{16,8},{24,16},{0,24},{9,1},{17,9},{25,17},{1,25},{10,2},{18... | collective-permute-start | bytes 294920 | tf_op jit(solution)/shard_map/ppermute | solution.py:19
  10.2 3.4 %copy-start.4 = (f32[256]{0:T(256)S(1)}, f32[256]{0:T(256)}, u32[]{:S(2)}) copy-start(f32[256]{0:T(256)} %param.12) | copy-start | bytes 3076
  10.2 14.8 %copy-start.2 = (f32[3,4,32,8,256]{4,3,2,1,0:T(8,128)S(1)}, f32[3,4,32,8,256]{4,3,2,1,0:T(8,128)}, u32[]{:S(2)}) copy-start(f32[3,4,32,8,256]{4,3,2,1,0:T(8,128)} %param.11) | copy-start | bytes 9437188
  13.1 9.0 %collective-permute-start.2 = (f32[3,4,34,1,256]{4,3,2,1,0:T(1,128)S(1)}, f32[3,4,34,1,256]{4,3,2,1,0:T(1,128)S(1)}, u32[]{:S(2)}, u32[]{:S(2)}) collective-permute-start(f32[3,4,34,1,256]{4,3,2,1,0:T(1,128)S(1)} %get-tuple-element.75), channel_id=1, source_target_pairs={{2,0},{4,2},{6,4},{0,6},{3,1},{5,3},{7,5},{1,7},{10,8},{12,10},{14... | collective-permute-start | bytes 1253384 | tf_op jit(solution)/shard_map/ppermute | solution.py:19
  13.1 11.9 %collective-permute-start.3 = (f32[3,4,34,1,256]{4,3,2,1,0:T(1,128)S(1)}, f32[3,4,34,1,256]{4,3,2,1,0:T(1,128)S(1)}, u32[]{:S(2)}, u32[]{:S(2)}) collective-permute-start(f32[3,4,34,1,256]{4,3,2,1,0:T(1,128)S(1)} %get-tuple-element.76), channel_id=1, source_target_pairs={{0,2},{2,4},{4,6},{6,0},{1,3},{3,5},{5,7},{7,1},{8,10},{10,12},{12... | collective-permute-start | bytes 1253384 | tf_op jit(solution)/shard_map/ppermute | solution.py:17
  30.5 6.6 %collective-permute-start.4 = (f32[3,4,1,8,256]{4,3,2,1,0:T(8,128)S(1)}, f32[3,4,1,8,256]{4,3,2,1,0:T(8,128)S(1)}, u32[]{:S(2)}, u32[]{:S(2)}) collective-permute-start(f32[3,4,1,8,256]{4,3,2,1,0:T(8,128)S(1)} %get-tuple-element.84), channel_id=1, source_target_pairs={{8,0},{16,8},{24,16},{0,24},{9,1},{17,9},{25,17},{1,25},{10,2},{18... | collective-permute-start | bytes 294920 | tf_op jit(solution)/shard_map/ppermute | solution.py:19
  33.9 6.4 %collective-permute-start.5 = (f32[3,4,1,8,256]{4,3,2,1,0:T(8,128)S(1)}, f32[3,4,1,8,256]{4,3,2,1,0:T(8,128)S(1)}, u32[]{:S(2)}, u32[]{:S(2)}) collective-permute-start(f32[3,4,1,8,256]{4,3,2,1,0:T(8,128)S(1)} %get-tuple-element.83), channel_id=1, source_target_pairs={{0,8},{8,16},{16,24},{24,0},{1,9},{9,17},{17,25},{25,1},{2,10},{10... | collective-permute-start | bytes 294920 | tf_op jit(solution)/shard_map/ppermute | solution.py:17
  40.8 9.9 %collective-permute-start.6 = (f32[3,4,34,1,256]{4,3,2,1,0:T(1,128)S(1)}, f32[3,4,34,1,256]{4,3,2,1,0:T(1,128)S(1)}, u32[]{:S(2)}, u32[]{:S(2)}) collective-permute-start(f32[3,4,34,1,256]{4,3,2,1,0:T(1,128)S(1)} %get-tuple-element.73), channel_id=1, source_target_pairs={{2,0},{4,2},{6,4},{0,6},{3,1},{5,3},{7,5},{1,7},{10,8},{12,10},{14... | collective-permute-start | bytes 1253384 | tf_op jit(solution)/shard_map/ppermute | solution.py:19
  40.8 11.0 %collective-permute-start.7 = (f32[3,4,34,1,256]{4,3,2,1,0:T(1,128)S(1)}, f32[3,4,34,1,256]{4,3,2,1,0:T(1,128)S(1)}, u32[]{:S(2)}, u32[]{:S(2)}) collective-permute-start(f32[3,4,34,1,256]{4,3,2,1,0:T(1,128)S(1)} %get-tuple-element.74), channel_id=1, source_target_pairs={{0,2},{2,4},{4,6},{6,0},{1,3},{3,5},{5,7},{7,1},{8,10},{10,12},{12... | collective-permute-start | bytes 1253384 | tf_op jit(solution)/shard_map/ppermute | solution.py:17
  60.3 5.7 %collective-permute-start.8 = (f32[3,4,1,8,256]{4,3,2,1,0:T(8,128)S(1)}, f32[3,4,1,8,256]{4,3,2,1,0:T(8,128)S(1)}, u32[]{:S(2)}, u32[]{:S(2)}) collective-permute-start(f32[3,4,1,8,256]{4,3,2,1,0:T(8,128)S(1)} %get-tuple-element.82), channel_id=1, source_target_pairs={{8,0},{16,8},{24,16},{0,24},{9,1},{17,9},{25,17},{1,25},{10,2},{18... | collective-permute-start | bytes 294920 | tf_op jit(solution)/shard_map/ppermute | solution.py:19
  61.0 6.4 %collective-permute-start.9 = (f32[3,4,1,8,256]{4,3,2,1,0:T(8,128)S(1)}, f32[3,4,1,8,256]{4,3,2,1,0:T(8,128)S(1)}, u32[]{:S(2)}, u32[]{:S(2)}) collective-permute-start(f32[3,4,1,8,256]{4,3,2,1,0:T(8,128)S(1)} %get-tuple-element.81), channel_id=1, source_target_pairs={{0,8},{8,16},{16,24},{24,0},{1,9},{9,17},{17,25},{25,1},{2,10},{10... | collective-permute-start | bytes 294920 | tf_op jit(solution)/shard_map/ppermute | solution.py:17
  67.9 9.0 %collective-permute-start.10 = (f32[3,4,34,1,256]{4,3,2,1,0:T(1,128)S(1)}, f32[3,4,34,1,256]{4,3,2,1,0:T(1,128)S(1)}, u32[]{:S(2)}, u32[]{:S(2)}) collective-permute-start(f32[3,4,34,1,256]{4,3,2,1,0:T(1,128)S(1)} %get-tuple-element.71), channel_id=1, source_target_pairs={{2,0},{4,2},{6,4},{0,6},{3,1},{5,3},{7,5},{1,7},{10,8},{12,10},{14... | collective-permute-start | bytes 1253384 | tf_op jit(solution)/shard_map/ppermute | solution.py:19
  68.0 11.9 %collective-permute-start.11 = (f32[3,4,34,1,256]{4,3,2,1,0:T(1,128)S(1)}, f32[3,4,34,1,256]{4,3,2,1,0:T(1,128)S(1)}, u32[]{:S(2)}, u32[]{:S(2)}) collective-permute-start(f32[3,4,34,1,256]{4,3,2,1,0:T(1,128)S(1)} %get-tuple-element.72), channel_id=1, source_target_pairs={{0,2},{2,4},{4,6},{6,0},{1,3},{3,5},{5,7},{7,1},{8,10},{10,12},{12... | collective-permute-start | bytes 1253384 | tf_op jit(solution)/shard_map/ppermute | solution.py:17
  85.6 4.9 %collective-permute-start.12 = (f32[3,4,1,8,256]{4,3,2,1,0:T(8,128)S(1)}, f32[3,4,1,8,256]{4,3,2,1,0:T(8,128)S(1)}, u32[]{:S(2)}, u32[]{:S(2)}) collective-permute-start(f32[3,4,1,8,256]{4,3,2,1,0:T(8,128)S(1)} %get-tuple-element.80), channel_id=1, source_target_pairs={{8,0},{16,8},{24,16},{0,24},{9,1},{17,9},{25,17},{1,25},{10,2},{18... | collective-permute-start | bytes 294920 | tf_op jit(solution)/shard_map/ppermute | solution.py:19
  86.5 6.6 %collective-permute-start.13 = (f32[3,4,1,8,256]{4,3,2,1,0:T(8,128)S(1)}, f32[3,4,1,8,256]{4,3,2,1,0:T(8,128)S(1)}, u32[]{:S(2)}, u32[]{:S(2)}) collective-permute-start(f32[3,4,1,8,256]{4,3,2,1,0:T(8,128)S(1)} %get-tuple-element.79), channel_id=1, source_target_pairs={{0,8},{8,16},{16,24},{24,0},{1,9},{9,17},{17,25},{25,1},{2,10},{10... | collective-permute-start | bytes 294920 | tf_op jit(solution)/shard_map/ppermute | solution.py:17
  93.6 9.7 %collective-permute-start.14 = (f32[3,4,34,1,256]{4,3,2,1,0:T(1,128)S(1)}, f32[3,4,34,1,256]{4,3,2,1,0:T(1,128)S(1)}, u32[]{:S(2)}, u32[]{:S(2)}) collective-permute-start(f32[3,4,34,1,256]{4,3,2,1,0:T(1,128)S(1)} %get-tuple-element.69), channel_id=1, source_target_pairs={{2,0},{4,2},{6,4},{0,6},{3,1},{5,3},{7,5},{1,7},{10,8},{12,10},{14... | collective-permute-start | bytes 1253384 | tf_op jit(solution)/shard_map/ppermute | solution.py:19
  94.0 11.7 %collective-permute-start.15 = (f32[3,4,34,1,256]{4,3,2,1,0:T(1,128)S(1)}, f32[3,4,34,1,256]{4,3,2,1,0:T(1,128)S(1)}, u32[]{:S(2)}, u32[]{:S(2)}) collective-permute-start(f32[3,4,34,1,256]{4,3,2,1,0:T(1,128)S(1)} %get-tuple-element.70), channel_id=1, source_target_pairs={{0,2},{2,4},{4,6},{6,0},{1,3},{3,5},{5,7},{7,1},{8,10},{10,12},{12... | collective-permute-start | bytes 1253384 | tf_op jit(solution)/shard_map/ppermute | solution.py:17
  109.4 70.1 %collective-permute-start.16 = (f32[3,4,32,8,256]{4,3,2,1,0:T(8,128)S(1)}, f32[3,4,32,8,256]{4,3,2,1,0:T(8,128)}, u32[]{:S(2)}, u32[]{:S(2)}) collective-permute-start(f32[3,4,32,8,256]{4,3,2,1,0:T(8,128)S(1)} %get-tuple-element.78), channel_id=1, source_target_pairs={{0,1},{1,0},{2,3},{3,2},{4,5},{5,4},{6,7},{7,6},{8,9},{9,8},{10,11... | collective-permute-start | bytes 9437192 | tf_op jit(solution)/shard_map/ppermute | solution.py:115
  184.1 4.5 %copy-start.3 = (f32[3,16,32,8,256]{4,3,2,1,0:T(8,128)}, f32[3,16,32,8,256]{4,3,2,1,0:T(8,128)S(1)}, u32[]{:S(2)}) copy-start(f32[3,16,32,8,256]{4,3,2,1,0:T(8,128)S(1)} %pad_maximum_fusion) | copy-start | bytes 37748740
  315.5 13.5 %copy-start.1 = (f32[256,256]{1,0:T(8,128)S(1)}, f32[256,256]{1,0:T(8,128)}, u32[]{:S(2)}) copy-start(f32[256,256]{1,0:T(8,128)} %param.13) | copy-start | bytes 786436
